TPU v7x, 32 devices: a whole 2x2x4 slice. The times are simulated.
32 devices in a mesh: dp: 4 (over y, x), expert: 8 (over z, core).
Axes of the slice: x: 2, y: 2, z: 4, core: 2. Of those that a mesh axis runs over, the one named last changes fastest.
Arguments:
- tokens: bfloat16 [4096, 7168], P(('dp', 'expert')), may hold values from -6 to 6
- cotangent: bfloat16 [4096, 7168], P(('dp', 'expert')), may hold values from -6 to 6
- route_ids: int32 [4096, 8], P(('dp', 'expert')), may hold values from 0 to 31, all different within a row; in each aligned block of 128 rows (0 to 127, 128 to 255, ...) at most 40 rows name the same one
- router_weights: float32 [4096, 8], P(('dp', 'expert')), may hold values from 0.05 to 0.3
- master: float32 [8, 7168, 384], P('expert', 'dp'), may hold values from -0.0625 to 0.0625
- accumulator: float32 [8, 3, 7168], P('expert', None, 'dp'), may hold values from 0.1 to 10
Outputs:
- output: bfloat16 [4096, 7168], P(('dp', 'expert'))
- input_grad: bfloat16 [4096, 7168], P(('dp', 'expert'))
- new_weights: bfloat16 [8, 7168, 384], P('expert', 'dp')
- accumulator_out: float32 [8, 3, 7168], P('expert', None, 'dp')
Inputs may be any that keep to these rules, and one draw needn't show every extreme that they name: `route_ids`: each row names distinct experts. In each aligned block of 128 rows (the rows of one device) no expert is named by more than 40 rows, a bound that some block reaches.
All inputs are finite; a program needn't handle non-finite values.
Results may differ from a plain program's by a relative error of at most 0.011.
Values may be sent and summed in bfloat16 or wider, within the bound.
A program may use at most 128 MiB of HBM per device.

v0:
```python
import jax
import jax.numpy as jnp
from jax import lax
from jax.sharding import PartitionSpec as P

SLICES = 8
TOP = 8
EXP_DEV = 4


LEARN_RATE = 0.01
EPSILON = 1e-06


def from_partner(array, axis, bit):
    return lax.ppermute(array, axis, [(i, i ^ 1 << bit) for i in range(lax.axis_size(axis))])


def slot_table(block_ids, live_count, capacity):
    flat_ids = block_ids.reshape(-1)
    onehot = (flat_ids[:, None] == jnp.arange(live_count, dtype=jnp.int32)[None, :]).astype(
        jnp.int32
    )
    before = jnp.cumsum(onehot, axis=0) - onehot
    position = jnp.sum(before * onehot, axis=1)
    return jnp.where(flat_ids < live_count, flat_ids * capacity + position, live_count * capacity)


def contract_rows(left, right):
    return lax.dot_general(
        left, right, (((0,), (0,)), ((), ())), preferred_element_type=jnp.float32
    )


def contract_cols(left, right):
    return lax.dot_general(
        left, right, (((1,), (1,)), ((), ())), preferred_element_type=jnp.float32
    )


def forward_rows(in_rows, weights, slice_width):
    gate_up = jnp.dot(in_rows, weights[:, : 2 * slice_width], preferred_element_type=jnp.float32)
    gate_pre = gate_up[:, :slice_width]
    up_pre = gate_up[:, slice_width:]
    sigmoid_gate = jax.nn.sigmoid(gate_pre)
    silu_gate = gate_pre * sigmoid_gate
    hidden = (silu_gate * up_pre).astype(jnp.bfloat16)
    out_part = contract_cols(hidden, weights[:, 2 * slice_width :]).astype(jnp.bfloat16)
    return (hidden, out_part, (up_pre, sigmoid_gate, silu_gate, gate_pre))


def backward_rows(cot_rows, weights, slice_width, saved):
    up_pre, sigmoid_gate, silu_gate, gate_pre = saved
    grad_hidden = jnp.dot(
        cot_rows, weights[:, 2 * slice_width :], preferred_element_type=jnp.float32
    )
    grad_gate = grad_hidden * up_pre * sigmoid_gate * (1.0 + gate_pre * (1.0 - sigmoid_gate))
    grad_up = grad_hidden * silu_gate
    grad_pre = jnp.concatenate([grad_gate, grad_up], axis=1).astype(jnp.bfloat16)
    in_part = contract_cols(grad_pre, weights[:, : 2 * slice_width]).astype(jnp.bfloat16)
    return (grad_pre, in_part)


def local(tokens, cotangent, route_ids, router_weights, master, accumulator):
    devices_e = lax.axis_size("expert")
    live_count = devices_e // SLICES
    tok_rows = tokens.shape[0]
    model_width = tokens.shape[1]
    experts = EXP_DEV * devices_e
    capacity = max(2, 5 * tok_rows * TOP // (4 * experts))
    slice_width = master.shape[2] // 3
    quarter = master.shape[1]
    width = live_count * capacity
    own_master = master[0].astype(jnp.bfloat16)
    partner_rows = from_partner(own_master, "expert", 0)
    weights = lax.all_gather(partner_rows, "dp", axis=0, tiled=True)
    slot_ids = slot_table(route_ids, live_count, capacity)
    token_of = jnp.repeat(jnp.arange(tok_rows, dtype=jnp.int32), TOP)
    slot_token = jnp.zeros((width + 1,), jnp.int32).at[slot_ids].set(token_of)[:width]
    slot_weight = (
        jnp.zeros((width + 1,), jnp.float32).at[slot_ids].set(router_weights.reshape(-1))[:width]
    )
    filled = jnp.zeros((width + 1,), jnp.float32).at[slot_ids].set(1.0)[:width]
    token_rows = jnp.where(filled[:, None] > 0, tokens[slot_token], jnp.zeros((), jnp.bfloat16))
    grad_rows = (cotangent[slot_token].astype(jnp.float32) * slot_weight[:, None]).astype(
        jnp.bfloat16
    )

    def spread(rows):
        tiled = jnp.broadcast_to(
            rows.reshape(live_count, 1, capacity, model_width),
            (live_count, SLICES, capacity, model_width),
        )
        return tiled.reshape(devices_e, capacity, model_width)

    send_tokens = spread(token_rows)
    send_grads = spread(grad_rows)
    recv_tokens = lax.all_to_all(send_tokens, "expert", split_axis=0, concat_axis=0, tiled=True)
    in_rows = recv_tokens.reshape(-1, model_width)
    hidden, out_part, saved = forward_rows(in_rows, weights, slice_width)
    back_out = lax.all_to_all(
        out_part.reshape(devices_e, capacity, model_width),
        "expert",
        split_axis=0,
        concat_axis=0,
        tiled=True,
    )
    recv_grads = lax.all_to_all(send_grads, "expert", split_axis=0, concat_axis=0, tiled=True)
    cot_rows = recv_grads.reshape(-1, model_width)
    grad_pre, in_part = backward_rows(cot_rows, weights, slice_width, saved)
    back_in = lax.all_to_all(
        in_part.reshape(devices_e, capacity, model_width),
        "expert",
        split_axis=0,
        concat_axis=0,
        tiled=True,
    )
    grad_in = contract_rows(in_rows, grad_pre)
    grad_down = contract_rows(cot_rows, hidden)
    summed = lax.psum_scatter(
        jnp.concatenate([grad_in, grad_down], axis=1).astype(jnp.bfloat16),
        "dp",
        scatter_dimension=0,
        tiled=True,
    )
    held_grad = from_partner(summed, "expert", 0)
    slot_index = jnp.arange(width, dtype=jnp.int32)
    recv_index = jnp.arange(devices_e * capacity, dtype=jnp.int32)
    same_expert = slot_index[:, None] // capacity == recv_index[None, :] // (SLICES * capacity)
    same_place = slot_index[:, None] % capacity == recv_index[None, :] % capacity
    merge = jnp.where(same_expert & same_place, 1.0, 0.0).astype(jnp.bfloat16)
    out_sum = jnp.dot(merge, back_out.reshape(-1, model_width), preferred_element_type=jnp.float32)
    in_sum = jnp.dot(merge, back_in.reshape(-1, model_width), preferred_element_type=jnp.float32)
    pick_slots = slot_ids.reshape(tok_rows, TOP)
    hits = jnp.sum(
        (pick_slots[:, :, None] == slot_index[None, None, :]).astype(jnp.float32), axis=1
    )
    high = lax.Precision.HIGHEST
    output = jnp.dot(hits * slot_weight[None, :], out_sum, precision=high).astype(jnp.bfloat16)
    input_grad = jnp.dot(hits, in_sum, precision=high).astype(jnp.bfloat16)
    grad_full = held_grad.astype(jnp.float32).reshape(quarter, 3, slice_width)
    mean_square = jnp.mean(grad_full * grad_full, axis=2)
    accumulator_out = accumulator[0] + mean_square.T
    scale = 1.0 / (jnp.sqrt(accumulator_out) + EPSILON)
    update = grad_full * scale.T[:, :, None]
    master_new = master[0] - LEARN_RATE * update.reshape(quarter, 3 * slice_width)
    returned = from_partner(master_new.astype(jnp.bfloat16), "expert", 0)
    return (output, input_grad, returned[None], accumulator_out[None])


def solution(mesh):
    return jax.shard_map(
        local,
        mesh=mesh,
        in_specs=(
            P(("dp", "expert"), None),
            P(("dp", "expert"), None),
            P(("dp", "expert"), None),
            P(("dp", "expert"), None),
            P("expert", "dp", None),
            P("expert", None, "dp"),
        ),
        out_specs=(
            P(("dp", "expert"), None),
            P(("dp", "expert"), None),
            P("expert", "dp", None),
            P("expert", None, "dp"),
        ),
        check_vma=False,
    )
```

profile of v0, /device:TPU:9, one launch (start us, length us, event | category | flops | bytes accessed | tf_op | source)
XLA Modules:
  0.0 475.9 jit_solution(14403577457215705809)
XLA Ops:
  7.2 0.0 copy-start
  7.2 0.9 copy.20
  8.1 0.1 reshape.322
  8.2 0.3 reduce-window.6
  8.5 0.2 slice_reduce_fusion
  8.7 0.1 reshape.306
  8.8 0.1 reshape.359
  8.9 0.2 reduce-window.9
  9.1 0.1 eq.92
  9.2 0.1 broadcast.217
  9.2 0.1 reshape.309
  9.4 0.1 lt.48
  9.5 0.1 mul.92
  9.6 4.3 scatter_custom_fusion.2
  13.9 4.3 scatter_custom_fusion.1
  18.3 0.0 copy-done
  18.3 0.9 gather_fusion
  19.2 0.1 broadcast_select_fusion
  19.3 2.7 reshape.314
  22.0 5.6 %all-to-all-start = ((bf16[8,40,7168]{2,1,0:T(8,128)(2,1)}), bf16[8,40,7168]{2,1,0:T(8,128)(2,1)}, u32[]{:S(2)}, u32[]{:S(2)}) async-start(bf16[8,40,7168]{2,1,0:T(8,128)(2,1)} %reshape.314), calls=%async_computation | async-start | bytes 9175040 | tf_op jit(solution)/shard_map/all_to_all | solution.py:98
  27.6 0.0 all-gather.2.cloned.1.call-start
  27.6 2.2 copy.25
  29.9 1.2 bitcast_convert_fusion
  31.1 0.4 collective-permute-start
  31.5 0.0 copy-done.4
  31.5 0.1 copy.24
  31.6 0.1 reshape.343
  31.7 4.3 scatter_custom_fusion
  36.0 4.0 gather_fusion.1
  40.0 0.0 collective-permute-done
  40.0 0.0 all-gather.2.cloned.1.call-update
  40.0 1.2 multiply_convert_fusion
  41.2 85.3 %all-to-all-done = bf16[8,40,7168]{2,1,0:T(8,128)(2,1)} async-done(((bf16[8,40,7168]{2,1,0:T(8,128)(2,1)}), bf16[8,40,7168]{2,1,0:T(8,128)(2,1)}, u32[]{:S(2)}, u32[]{:S(2)}) %all-to-all-start) | async-done | bytes 4587552 | tf_op jit(solution)/shard_map/all_to_all | solution.py:98
  126.5 2.7 reshape.318
  129.2 8.1 %all-to-all-start.2 = ((bf16[8,40,7168]{2,1,0:T(8,128)(2,1)}), bf16[8,40,7168]{2,1,0:T(8,128)(2,1)}, u32[]{:S(2)}, u32[]{:S(2)}) async-start(bf16[8,40,7168]{2,1,0:T(8,128)(2,1)} %reshape.318), calls=%async_computation.2 | async-start | bytes 9175040 | tf_op jit(solution)/shard_map/all_to_all | solution.py:108
  137.3 4.8 %fusion.1 = f32[320,256]{1,0:T(8,128)S(1)} fusion(bf16[320,7168]{1,0:T(8,128)(2,1)} %bitcast.4, bf16[7168,384]{0,1:T(8,128)(2,1)} %all-gather.2.cloned.1.call-done), kind=kOutput, calls=%fused_computation.15 | convolution fusion | flops 1174405120 | bytes 8585216 | tf_op jit(solution)/shard_map/dot_general | solution.py:42
  142.2 94.1 %all-to-all-done.2 = bf16[8,40,7168]{2,1,0:T(8,128)(2,1)} async-done(((bf16[8,40,7168]{2,1,0:T(8,128)(2,1)}), bf16[8,40,7168]{2,1,0:T(8,128)(2,1)}, u32[]{:S(2)}, u32[]{:S(2)}) %all-to-all-start.2) | async-done | bytes 4587552 | tf_op jit(solution)/shard_map/all_to_all | solution.py:108
  236.2 4.4 multiply_convert_fusion.2
  240.6 0.1 copy-done.2
  240.7 3.5 convolution_convert_fusion
  244.2 8.1 %all-to-all-start.3 = ((bf16[8,40,7168]{2,1,0:T(8,128)(2,1)}), bf16[8,40,7168]{2,1,0:T(8,128)(2,1)}, u32[]{:S(2)}, u32[]{:S(2)}) async-start(bf16[8,40,7168]{2,1,0:T(8,128)(2,1)} %bitcast.45), calls=%async_computation.3 | async-start | bytes 9175040 | tf_op jit(solution)/shard_map/all_to_all | solution.py:111
  252.3 0.0 reduce-scatter.2.cloned.1.call-start
  252.3 3.5 convolution_convert_fusion.3
  255.8 4.4 convolution_convert_fusion.2
  260.2 2.8 pad_maximum_fusion
  263.0 0.0 reduce-scatter.2.cloned.1.call-update
  263.0 4.9 %convolution_convert_fusion.1 = bf16[320,7168]{1,0:T(8,128)(2,1)} fusion(bf16[320,128]{1,0:T(8,128)(2,1)S(1)} %get-tuple-element.24, bf16[7168,384]{0,1:T(8,128)(2,1)} %all-gather.2.cloned.1.call-done), kind=kOutput, calls=%fused_computation.6 | convolution fusion | flops 589496320 | bytes 6504448 | tf_op jit(solution)/shard_map/dot_general | solution.py:36
  267.9 83.3 %all-to-all-done.3 = bf16[8,40,7168]{2,1,0:T(8,128)(2,1)} async-done(((bf16[8,40,7168]{2,1,0:T(8,128)(2,1)}), bf16[8,40,7168]{2,1,0:T(8,128)(2,1)}, u32[]{:S(2)}, u32[]{:S(2)}) %all-to-all-start.3) | async-done | bytes 4587552 | tf_op jit(solution)/shard_map/all_to_all | solution.py:111
  351.2 8.1 %all-to-all-start.1 = ((bf16[8,40,7168]{2,1,0:T(8,128)(2,1)}), bf16[8,40,7168]{2,1,0:T(8,128)(2,1)}, u32[]{:S(2)}, u32[]{:S(2)}) async-start(bf16[8,40,7168]{2,1,0:T(8,128)(2,1)} %bitcast.44), calls=%async_computation.1 | async-start | bytes 9175040 | tf_op jit(solution)/shard_map/all_to_all | solution.py:101
  359.3 0.4 collective-permute-start.1
  359.8 3.7 collective-permute-done.1
  363.4 3.1 convert_multiply_fusion.1
  366.5 1.9 reduce_sum.20
  368.5 0.0 copy-done.3
  368.5 2.8 fusion.5
  371.3 0.1 collective-permute-start.2
  371.5 3.2 fusion.11
  374.7 4.2 convolution_convert_fusion.4
  378.9 79.3 %all-to-all-done.1 = bf16[8,40,7168]{2,1,0:T(8,128)(2,1)} async-done(((bf16[8,40,7168]{2,1,0:T(8,128)(2,1)}), bf16[8,40,7168]{2,1,0:T(8,128)(2,1)}, u32[]{:S(2)}, u32[]{:S(2)}) %all-to-all-start.1) | async-done | bytes 4587552 | tf_op jit(solution)/shard_map/all_to_all | solution.py:101
  458.2 3.4 fusion.12
  461.5 4.4 convolution_convert_fusion.5
  465.9 0.6 broadcast_in_dim.68
  466.5 0.0 collective-permute-done.2
  466.5 2.5 copy.26
  (21 shorter events, 0.2 us)
Async XLA Ops:
  7.2 11.1 %copy-start = (bf16[128,7168]{1,0:T(8,128)(2,1)S(1)}, bf16[128,7168]{1,0:T(8,128)(2,1)}, u32[]{:S(2)}) copy-start(bf16[128,7168]{1,0:T(8,128)(2,1)} %param.6) | copy-start | bytes 5505028
  22.0 104.5 %all-to-all-start = ((bf16[8,40,7168]{2,1,0:T(8,128)(2,1)}), bf16[8,40,7168]{2,1,0:T(8,128)(2,1)}, u32[]{:S(2)}, u32[]{:S(2)}) async-start(bf16[8,40,7168]{2,1,0:T(8,128)(2,1)} %reshape.314), calls=%async_computation | async-start | bytes 9175040 | tf_op jit(solution)/shard_map/all_to_all | solution.py:98
  27.6 3.9 copy-start.4
  27.6 109.7 %all-gather.2.cloned.1.call-start = ((), (), s32[]{:S(2)}) async-start(), calls=%async_computation.5 | async-start | bytes 6881280 | tf_op jit(solution)/shard_map/all_gather | solution.py:76
  31.1 8.9 %collective-permute-start = (bf16[1792,384]{0,1:T(8,128)(2,1)}, bf16[1792,384]{0,1:T(8,128)(2,1)}, u32[]{:S(2)}, u32[]{:S(2)}) collective-permute-start(bf16[1792,384]{0,1:T(8,128)(2,1)} %bitcast_convert_fusion), channel_id=1, source_target_pairs={{0,1},{1,0},{2,3},{3,2},{4,5},{5,4},{6,7},{7,6},{8,9},{9,8},{10,11... | collective-permute-start | bytes 4128776 | tf_op jit(solution)/shard_map/ppermute | solution.py:16
  129.2 107.0 %all-to-all-start.2 = ((bf16[8,40,7168]{2,1,0:T(8,128)(2,1)}), bf16[8,40,7168]{2,1,0:T(8,128)(2,1)}, u32[]{:S(2)}, u32[]{:S(2)}) async-start(bf16[8,40,7168]{2,1,0:T(8,128)(2,1)} %reshape.318), calls=%async_computation.2 | async-start | bytes 9175040 | tf_op jit(solution)/shard_map/all_to_all | solution.py:108
  236.2 4.5 copy-start.2
  244.2 107.0 %all-to-all-start.3 = ((bf16[8,40,7168]{2,1,0:T(8,128)(2,1)}), bf16[8,40,7168]{2,1,0:T(8,128)(2,1)}, u32[]{:S(2)}, u32[]{:S(2)}) async-start(bf16[8,40,7168]{2,1,0:T(8,128)(2,1)} %bitcast.45), calls=%async_computation.3 | async-start | bytes 9175040 | tf_op jit(solution)/shard_map/all_to_all | solution.py:111
  252.3 107.0 %reduce-scatter.2.cloned.1.call-start = ((), (), s32[]{:S(2)}) async-start(), calls=%async_computation.6 | async-start | bytes 6881280 | tf_op jit(solution)/shard_map/reduce_scatter | solution.py:120
  351.2 107.0 %all-to-all-start.1 = ((bf16[8,40,7168]{2,1,0:T(8,128)(2,1)}), bf16[8,40,7168]{2,1,0:T(8,128)(2,1)}, u32[]{:S(2)}, u32[]{:S(2)}) async-start(bf16[8,40,7168]{2,1,0:T(8,128)(2,1)} %bitcast.44), calls=%async_computation.1 | async-start | bytes 9175040 | tf_op jit(solution)/shard_map/all_to_all | solution.py:101
  359.3 9.2 %copy-start.3 = (f32[1,3,1792]{2,0,1:T(1,128)S(1)}, f32[1,3,1792]{2,0,1:T(1,128)}, u32[]{:S(2)}) copy-start(f32[1,3,1792]{2,0,1:T(1,128)} %param.11) | copy-start | bytes 64516
  359.3 4.2 collective-permute-start.1
  371.3 95.2 %collective-permute-start.2 = (bf16[1792,384]{0,1:T(8,128)(2,1)}, bf16[1792,384]{0,1:T(8,128)(2,1)}, u32[]{:S(2)}, u32[]{:S(2)}) collective-permute-start(bf16[1792,384]{0,1:T(8,128)(2,1)} %fusion.5), channel_id=1, source_target_pairs={{0,1},{1,0},{2,3},{3,2},{4,5},{5,4},{6,7},{7,6},{8,9},{9,8},{10,11... | collective-permute-start | bytes 4128776 | tf_op jit(solution)/shard_map/ppermute | solution.py:16
  458.2 10.8 %copy-start.1 = (bf16[128,7168]{1,0:T(8,128)(2,1)S(1)}, bf16[128,7168]{1,0:T(8,128)(2,1)}, u32[]{:S(2)}) copy-start(bf16[128,7168]{1,0:T(8,128)(2,1)} %param.6) | copy-start | bytes 5505028
Sparse Core Ops, SparseCore 0:
  40.1 63.7 all-gather.1
  263.1 63.9 reduce-scatter.1
where the time goes:
time: 481 us; the launch traced here: 476 us
  waiting for transfers between devices  346 us (72%)
  matrix products  40.6 us (8%)
  local copies, waits for them, and re-layouts  30.8 us (6%)
  starting transfers between devices  30.8 us (6%)
  between operations  14.2 us (3%)
  other arithmetic  13.8 us (3%)
    all_to_all x1, waiting for transfers between devices, local(): lax.all_to_all(send_grads, 'expert', split_axis=0, concat_axis=0, tiled=T...  94.1 us
    all_to_all x1, waiting for transfers between devices, local(): lax.all_to_all(send_tokens, 'expert', split_axis=0, concat_axis=0, tiled=...  85.3 us
    all_to_all x1, waiting for transfers between devices, local(): lax.all_to_all(in_part.reshape(devices_e, capacity, model_width), 'expert...  83.3 us
    all_to_all x1, waiting for transfers between devices, local(): lax.all_to_all(out_part.reshape(devices_e, capacity, model_width), 'exper...  79.3 us
  transfers between devices with their start and end apart: 9, of which 5 were waited for; matrix products, arithmetic and copies ran while one was open for 13% of the time, Pallas kernels for 0%

commit v1 on v0

v1 whole, which is shorter than its diff:
```python
import jax
import jax.numpy as jnp
from jax import lax
from jax.sharding import Mesh
from jax.sharding import PartitionSpec as P

SLICES = 8
CORES = 2
EXP_DEV = 4

LEARN_RATE = 0.01
EPSILON = 1e-06


def swap(array):
    return lax.ppermute(array, "core", [(0, 1), (1, 0)])


def ordered(core, own, other, axis):
    first = jnp.where(core == 0, own, other)
    second = jnp.where(core == 0, other, own)
    return jnp.concatenate([first, second], axis=axis)


def slot_hits(block_ids, live_count, capacity):
    rows, top = block_ids.shape
    flat_ids = block_ids.reshape(-1)
    onehot = (flat_ids[:, None] == jnp.arange(live_count, dtype=jnp.int32)[None, :]).astype(
        jnp.int32
    )
    before = jnp.cumsum(onehot, axis=0) - onehot
    position = jnp.sum(before * onehot, axis=1)
    slots = jnp.where(flat_ids < live_count, flat_ids * capacity + position, live_count * capacity)
    slot_index = jnp.arange(live_count * capacity, dtype=jnp.int32)
    return slots.reshape(rows, top)[:, :, None] == slot_index[None, None, :]


def dot(left, right, left_dim, right_dim, precision=None):
    return lax.dot_general(
        left,
        right,
        (((left_dim,), (right_dim,)), ((), ())),
        preferred_element_type=jnp.float32,
        precision=precision,
    )


def local(tokens, cotangent, route_ids, router_weights, master, accumulator):
    devices_e = lax.axis_size("ex") * SLICES
    live_count = lax.axis_size("ex")
    chips = lax.axis_size("sl")
    replicas = lax.axis_size("dp")
    core = lax.axis_index("core")
    tok_rows = tokens.shape[0]
    model_width = tokens.shape[1]
    top = route_ids.shape[1]
    experts = EXP_DEV * devices_e
    capacity = max(2, 5 * tok_rows * top // (4 * experts))
    slice_width = master.shape[2] // 3
    quarter = master.shape[1]
    half = quarter // CORES
    width = live_count * capacity
    half_width = model_width // CORES
    bf16 = jnp.bfloat16

    def split_cols(rows):
        parts = rows.reshape(rows.shape[0], replicas, CORES, half)
        first = parts[:, :, 0].reshape(rows.shape[0], half_width)
        second = parts[:, :, 1].reshape(rows.shape[0], half_width)
        return jnp.where(core == 0, first, second), jnp.where(core == 0, second, first)

    def join_cols(own, other):
        first = jnp.where(core == 0, own, other)
        second = jnp.where(core == 0, other, own)
        shape = (own.shape[0], replicas, 1, half)
        return jnp.concatenate([first.reshape(shape), second.reshape(shape)], axis=2).reshape(
            own.shape[0], model_width
        )

    held = master[0].astype(bf16)
    held_low, held_high = held[:half], held[half:]
    held_mine = jnp.where(core == 0, held_low, held_high)
    held_other = jnp.where(core == 0, held_high, held_low)
    got = swap(held_other)
    slice_a = jnp.where(core == 0, got, held_mine)
    slice_b = jnp.where(core == 0, held_mine, got)
    two = 2 * slice_width
    paired = jnp.concatenate(
        [slice_a[:, :two], slice_b[:, :two], slice_a[:, two:], slice_b[:, two:]], axis=1
    )
    weights = lax.all_gather(paired, "dp", axis=0, tiled=True)
    w_in = weights[:, : 2 * two]
    w_down = weights[:, 2 * two :]

    picks = slot_hits(route_ids, live_count, capacity)
    hits = jnp.sum(picks.astype(jnp.float32), axis=1)
    slot_weight = jnp.sum(jnp.where(picks, router_weights[:, :, None], 0.0), axis=(0, 1))
    select = hits.astype(bf16)
    token_rows = dot(select, tokens, 0, 0).astype(bf16)
    grad_rows = (dot(select, cotangent, 0, 0) * slot_weight[:, None]).astype(bf16)

    def gather(rows):
        own, other = split_cols(rows)
        block = ordered(
            core,
            own.reshape(live_count, 1, capacity, half_width),
            swap(other).reshape(live_count, 1, capacity, half_width),
            1,
        )
        if live_count > 1:
            block = lax.all_to_all(block, "ex", split_axis=0, concat_axis=0, tiled=True)
        block = block.reshape(1, live_count * CORES * capacity, half_width)
        tiled = jnp.broadcast_to(block, (chips,) + block.shape[1:])
        full = lax.all_to_all(tiled, "sl", split_axis=0, concat_axis=0, tiled=True)
        return full.reshape(-1, half_width)

    def give_back(part):
        blocks = part.reshape(chips, live_count * CORES * capacity, half_width)
        back = lax.all_to_all(blocks, "sl", split_axis=0, concat_axis=0, tiled=True)
        summed = jnp.sum(back.astype(jnp.float32), axis=0).astype(bf16)
        summed = summed.reshape(live_count, CORES, capacity, half_width)
        if live_count > 1:
            summed = lax.all_to_all(summed, "ex", split_axis=0, concat_axis=0, tiled=True)
        low = summed[:, 0].reshape(width, half_width)
        high = summed[:, 1].reshape(width, half_width)
        own = jnp.where(core == 0, low, high)
        other = swap(jnp.where(core == 0, high, low))
        return join_cols(own, other)

    in_rows = gather(token_rows)
    cot_rows = gather(grad_rows)

    gate_up_part = dot(in_rows, w_in, 1, 0)
    gate_up = gate_up_part + swap(gate_up_part)
    gate_pre = jnp.concatenate(
        [gate_up[:, :slice_width], gate_up[:, two : two + slice_width]], axis=1
    )
    up_pre = jnp.concatenate(
        [gate_up[:, slice_width:two], gate_up[:, two + slice_width :]], axis=1
    )
    sigmoid_gate = jax.nn.sigmoid(gate_pre)
    silu_gate = gate_pre * sigmoid_gate
    hidden = (silu_gate * up_pre).astype(bf16)
    out_part = dot(hidden, w_down, 1, 1).astype(bf16)
    out_rows = give_back(out_part)

    grad_hidden_part = dot(cot_rows, w_down, 1, 0)
    grad_hidden = grad_hidden_part + swap(grad_hidden_part)
    grad_gate = grad_hidden * up_pre * sigmoid_gate * (1.0 + gate_pre * (1.0 - sigmoid_gate))
    grad_up = grad_hidden * silu_gate
    grad_pre = jnp.concatenate(
        [
            grad_gate[:, :slice_width],
            grad_up[:, :slice_width],
            grad_gate[:, slice_width:],
            grad_up[:, slice_width:],
        ],
        axis=1,
    ).astype(bf16)
    in_part = dot(grad_pre, w_in, 1, 1).astype(bf16)
    back_rows = give_back(in_part)

    grad_in = dot(in_rows, grad_pre, 0, 0).astype(bf16)
    grad_down = dot(cot_rows, hidden, 0, 0).astype(bf16)
    summed = lax.psum_scatter(
        jnp.concatenate([grad_in, grad_down], axis=1),
        "dp",
        scatter_dimension=0,
        tiled=True,
    )
    low = jnp.concatenate(
        [summed[:, :two], summed[:, 2 * two : 2 * two + slice_width]], axis=1
    )
    high = jnp.concatenate([summed[:, two : 2 * two], summed[:, 2 * two + slice_width :]], axis=1)
    mine = jnp.where(core == 0, high, low)
    theirs = swap(jnp.where(core == 0, low, high))
    held_grad = ordered(core, mine, theirs, 0)

    grad_full = held_grad.astype(jnp.float32).reshape(quarter, 3, slice_width)
    mean_square = jnp.mean(grad_full * grad_full, axis=2)
    accumulator_out = accumulator[0] + mean_square.T
    scale = 1.0 / (jnp.sqrt(accumulator_out) + EPSILON)
    update = grad_full * scale.T[:, :, None]
    master_new = master[0] - LEARN_RATE * update.reshape(quarter, 3 * slice_width)
    returned = swap(master_new.astype(bf16))

    high_precision = lax.Precision.HIGHEST
    output = dot(
        hits * slot_weight[None, :], out_rows.astype(jnp.float32), 1, 0, high_precision
    ).astype(bf16)
    input_grad = dot(select, back_rows, 1, 0).astype(bf16)
    return (output, input_grad, returned[None], accumulator_out[None])


def solution(mesh):
    replicas, devices_e = mesh.devices.shape
    fine = Mesh(
        mesh.devices.reshape(replicas, devices_e // SLICES, SLICES // CORES, CORES),
        ("dp", "ex", "sl", "core"),
    )
    expert = ("ex", "sl", "core")
    rows = P(("dp",) + expert, None)
    return jax.shard_map(
        local,
        mesh=fine,
        in_specs=(rows, rows, rows, rows, P(expert, "dp", None), P(expert, None, "dp")),
        out_specs=(rows, rows, P(expert, "dp", None), P(expert, None, "dp")),
        check_vma=False,
    )
```

time: 481 us -> 322 us (0.67)
  waiting for transfers between devices: 346 us -> 182 us
  other arithmetic: 13.8 us -> 26.3 us
  matrix products: 40.6 us -> 28.5 us
  starting transfers between devices: 30.8 us -> 37.2 us
    all_to_all x4, waiting for transfers between devices: 342 us -> 179 us  [the longest x2 91 us: gather(): full = lax.all_to_all(tiled, 'sl', split_axis=0, concat_axis=0, tiled=True)]
    scatter x3 -> x0, local copies, waits for them, and re-layouts: 12.9 us -> none  [the longest x1 4.3 us: local(): filled = jnp.zeros((width + 1,), jnp.float32).at[slot_ids].set(1.0)[:width]]
    dot_general x10, matrix products: 40.6 us -> 28.5 us  [dot(): lax.dot_general(left, right, (((left_dim,), (right_dim,)), ((), ())), pre...]
    select_n x6 -> x12, other arithmetic: 0.18 us -> 10.1 us  [the longest x2 2.72 us: ordered(): first = jnp.where(core == 0, own, other)]
    unnamed x14 -> x29, local copies, waits for them, and re-layouts: 5.87 us -> 15.7 us
    ppermute x3 -> x9, starting transfers between devices: 0.92 us -> 9.46 us  [swap(): return lax.ppermute(array, 'core', [(0, 1), (1, 0)])]
    gather x2 -> x0, local copies, waits for them, and re-layouts: 4.88 us -> none  [the longest x1 3.97 us: local(): cotangent[slot_token].astype(jnp.float32) * slot_weight[:, None]]
  transfers between devices with their start and end apart: 9 -> 15, of which waited for: 5 -> 6; matrix products, arithmetic and copies ran while one was open for 13% -> 18% of each run, Pallas kernels for 0% -> 0%
where the time goes in v1:
time: 322 us; the launch traced here: 317 us
  waiting for transfers between devices  182 us (57%)
  starting transfers between devices  37.2 us (12%)
  local copies, waits for them, and re-layouts  28.8 us (9%)
  matrix products  28.5 us (9%)
  other arithmetic  26.3 us (8%)
  between operations  14.5 us (5%)
    all_to_all x2, waiting for transfers between devices, gather(): full = lax.all_to_all(tiled, 'sl', split_axis=0, concat_axis=0, tiled=True)  91 us
    all_to_all x2, waiting for transfers between devices, give_back(): back = lax.all_to_all(blocks, 'sl', split_axis=0, concat_axis=0, tiled=True)  88.4 us
    dot_general x10, matrix products, dot(): lax.dot_general(left, right, (((left_dim,), (right_dim,)), ((), ())), pre...  28.5 us
    unnamed x29, local copies, waits for them, and re-layouts  15.7 us
    all_to_all x2, starting transfers between devices, give_back(): back = lax.all_to_all(blocks, 'sl', split_axis=0, concat_axis=0, tiled=True)  15.3 us
    all_to_all x2, starting transfers between devices, gather(): full = lax.all_to_all(tiled, 'sl', split_axis=0, concat_axis=0, tiled=True)  12.4 us
    ppermute x9, starting transfers between devices, swap(): return lax.ppermute(array, 'core', [(0, 1), (1, 0)])  9.46 us
  transfers between devices with their start and end apart: 15, of which 6 were waited for; matrix products, arithmetic and copies ran while one was open for 18% of the time, Pallas kernels for 0%

profile of v1, /device:TPU:9, one launch (start us, length us, event | category | flops | bytes accessed | tf_op | source)
XLA Modules:
  0.0 316.8 jit_solution(8676818178215987933)
XLA Ops:
  7.2 3.5 %copy.75 = f32[1,1792,384]{1,2,0:T(8,128)} copy(f32[1,1792,384]{2,1,0:T(8,128)} %param.10) | data formatting | bytes 5505024 | tf_op args[4]
  10.7 1.9 bitcast_convert_fusion
  12.6 0.9 broadcast_select_fusion.7
  13.6 0.7 collective-permute-start.1
  14.5 0.3 reduce-window.6
  15.7 1.2 fusion
  16.8 1.5 reshape.180
  18.4 0.8 fusion.22
  19.2 0.3 broadcast_select_fusion.9
  19.5 0.7 copy.97
  20.2 0.4 convolution_convert_fusion.2
  20.6 0.4 reshape.173
  21.1 1.3 broadcast_select_fusion.5
  22.5 1.2 pad_maximum_fusion.1
  23.7 0.8 fusion.23
  24.5 0.3 broadcast_select_fusion.11
  24.8 0.6 collective-permute-start
  25.5 1.1 collective-permute-done
  26.6 1.0 select_bitcast_fusion.2
  27.7 1.6 broadcast_in_dim.42
  29.3 4.8 %all-to-all-start = ((bf16[4,80,3584]{2,1,0:T(8,128)(2,1)}), bf16[4,80,3584]{2,1,0:T(8,128)(2,1)}, u32[]{:S(2)}, u32[]{:S(2)}) async-start(bf16[4,80,3584]{2,1,0:T(8,128)(2,1)} %broadcast_in_dim.42), calls=%async_computation | async-start | bytes 4587520 | tf_op jit(solution)/shard_map/all_to_all | solution.py:114
  34.1 48.8 %all-to-all-done = bf16[4,80,3584]{2,1,0:T(8,128)(2,1)} async-done(((bf16[4,80,3584]{2,1,0:T(8,128)(2,1)}), bf16[4,80,3584]{2,1,0:T(8,128)(2,1)}, u32[]{:S(2)}, u32[]{:S(2)}) %all-to-all-start) | async-done | bytes 2293792 | tf_op jit(solution)/shard_map/all_to_all | solution.py:114
  82.9 1.5 broadcast_in_dim.44
  84.4 7.7 %all-to-all-start.2 = ((bf16[4,80,3584]{2,1,0:T(8,128)(2,1)}), bf16[4,80,3584]{2,1,0:T(8,128)(2,1)}, u32[]{:S(2)}, u32[]{:S(2)}) async-start(bf16[4,80,3584]{2,1,0:T(8,128)(2,1)} %broadcast_in_dim.44), calls=%async_computation.2 | async-start | bytes 4587520 | tf_op jit(solution)/shard_map/all_to_all | solution.py:114
  92.1 4.2 %fusion.2 = f32[320,512]{1,0:T(8,128)S(1)} fusion(bf16[320,3584]{1,0:T(8,128)(2,1)} %bitcast.4, bf16[3584,768]{0,1:T(8,128)(2,1)} %all-gather.2.cloned.1.call-done), kind=kOutput, calls=%fused_computation.11 | convolution fusion | flops 1174405120 | bytes 6619136 | tf_op jit(solution)/shard_map/dot_general | solution.py:39
  96.3 1.8 collective-permute-start.2
  98.0 42.2 %all-to-all-done.2 = bf16[4,80,3584]{2,1,0:T(8,128)(2,1)} async-done(((bf16[4,80,3584]{2,1,0:T(8,128)(2,1)}), bf16[4,80,3584]{2,1,0:T(8,128)(2,1)}, u32[]{:S(2)}, u32[]{:S(2)}) %all-to-all-start.2) | async-done | bytes 2293792 | tf_op jit(solution)/shard_map/all_to_all | solution.py:114
  140.2 3.0 fusion.7
  143.2 2.3 collective-permute-start.5
  145.7 1.1 collective-permute-done.5
  147.0 2.8 convolution_convert_fusion.6
  149.8 3.7 %convolution_convert_fusion.3 = bf16[3584,512]{0,1:T(8,128)(2,1)S(1)} fusion(bf16[320,3584]{1,0:T(8,128)(2,1)} %bitcast.4, bf16[320,128]{1,0:T(8,128)(2,1)S(1)} %get-tuple-element.62, bf16[320,128]{1,0:T(8,128)(2,1)S(1)} %get-tuple-element.60, bf16[320,128]{1,0:T(8,128)(2,1)S(1)} %get-tuple-element.61, bf16[320,128]{1,0:T(8,128)(2,1)S(1)} %get-tuple-element.59), kind=kOutput, calls=%fused_computation.5 | convolution fusion | flops 1177550848 | bytes 6291456 | tf_op jit(solution)/shard_map/dot_general | solution.py:39
  153.6 2.7 pad_maximum_fusion
  156.3 8.0 %copy.83 = bf16[3584,768]{1,0:T(8,128)(2,1)} copy(bf16[3584,768]{0,1:T(8,128)(2,1)} %pad_maximum_fusion) | data formatting | bytes 11010048
  164.3 3.7 %convolution_convert_fusion.5 = bf16[320,3584]{1,0:T(8,128)(2,1)} fusion(bf16[320,256]{1,0:T(8,128)(2,1)S(1)} %get-tuple-element.46, bf16[3584,768]{0,1:T(8,128)(2,1)} %all-gather.2.cloned.1.call-done), kind=kOutput, calls=%fused_computation.8 | convolution fusion | flops 588349440 | bytes 4292608 | tf_op jit(solution)/shard_map/dot_general | solution.py:39
  168.0 7.7 %all-to-all-start.1 = ((bf16[4,80,3584]{2,1,0:T(8,128)(2,1)}), bf16[4,80,3584]{2,1,0:T(8,128)(2,1)}, u32[]{:S(2)}, u32[]{:S(2)}) async-start(bf16[4,80,3584]{2,1,0:T(8,128)(2,1)} %bitcast.80), calls=%async_computation.1 | async-start | bytes 4587520 | tf_op jit(solution)/shard_map/all_to_all | solution.py:119
  175.7 4.8 %convolution_convert_fusion.4 = bf16[320,3584]{1,0:T(8,128)(2,1)} fusion(bf16[3584,768]{0,1:T(8,128)(2,1)} %all-gather.2.cloned.1.call-done, bf16[320,128]{1,0:T(8,128)(2,1)S(1)} %get-tuple-element.62, bf16[320,128]{1,0:T(8,128)(2,1)S(1)} %get-tuple-element.60, bf16[320,128]{1,0:T(8,128)(2,1)S(1)} %get-tuple-element.61, ...), kind=kOutput, calls=%fused_computation.7 | convolution fusion | flops 1176862720 | bytes 6291456 | tf_op jit(solution)/shard_map/dot_general | solution.py:39
  180.5 44.4 %all-to-all-done.1 = bf16[4,80,3584]{2,1,0:T(8,128)(2,1)} async-done(((bf16[4,80,3584]{2,1,0:T(8,128)(2,1)}), bf16[4,80,3584]{2,1,0:T(8,128)(2,1)}, u32[]{:S(2)}, u32[]{:S(2)}) %all-to-all-start.1) | async-done | bytes 2293792 | tf_op jit(solution)/shard_map/all_to_all | solution.py:119
  224.9 7.5 %all-to-all-start.3 = ((bf16[4,80,3584]{2,1,0:T(8,128)(2,1)}), bf16[4,80,3584]{2,1,0:T(8,128)(2,1)}, u32[]{:S(2)}, u32[]{:S(2)}) async-start(bf16[4,80,3584]{2,1,0:T(8,128)(2,1)} %bitcast.87), calls=%async_computation.3 | async-start | bytes 4587520 | tf_op jit(solution)/shard_map/all_to_all | solution.py:119
  232.4 2.0 reduce_sum.57
  234.5 0.7 select_bitcast_fusion.3
  235.2 1.5 collective-permute-start.3
  236.7 44.0 %all-to-all-done.3 = bf16[4,80,3584]{2,1,0:T(8,128)(2,1)} async-done(((bf16[4,80,3584]{2,1,0:T(8,128)(2,1)}), bf16[4,80,3584]{2,1,0:T(8,128)(2,1)}, u32[]{:S(2)}, u32[]{:S(2)}) %all-to-all-start.3) | async-done | bytes 2293792 | tf_op jit(solution)/shard_map/all_to_all | solution.py:119
  280.7 2.0 reduce_sum.58
  282.8 0.7 select_bitcast_fusion
  283.5 2.1 collective-permute-start.6
  285.6 1.1 fusion.20
  286.9 1.3 fusion.19
  288.2 0.2 copy.92
  288.9 1.0 broadcast_select_fusion.2
  289.9 1.0 bitcast_select_fusion.3
  291.2 2.1 pad_maximum_fusion.5
  293.3 1.5 reshape.179
  294.8 1.7 broadcast_select_fusion.1
  296.5 0.3 multiply_reduce_fusion
  296.9 1.5 fusion.6
  298.4 0.5 collective-permute-start.8
  299.0 1.0 bitcast_select_fusion.1
  300.3 1.3 pad_maximum_fusion.7
  301.6 0.4 reshape.186
  302.0 1.9 convolution_convert_fusion
  303.9 2.9 convolution_convert_fusion.1
  306.9 0.6 broadcast_in_dim.46
  307.5 2.5 copy.82
  (68 shorter events, 3.1 us)
Async XLA Ops:
  7.2 8.5 %copy-start = (bf16[128,7168]{1,0:T(8,128)(2,1)S(1)}, bf16[128,7168]{1,0:T(8,128)(2,1)}, u32[]{:S(2)}) copy-start(bf16[128,7168]{1,0:T(8,128)(2,1)} %param.7) | copy-start | bytes 5505028
  7.2 84.9 %all-gather.2.cloned.1.call-start = ((), (), s32[]{:S(2)}) async-start(), calls=%async_computation.5 | async-start | bytes 6881280 | tf_op jit(solution)/shard_map/all_gather | solution.py:91
  10.7 3.6 %copy-start.7 = (s32[128,8]{0,1:T(8,128)S(1)}, s32[128,8]{0,1:T(8,128)}, u32[]{:S(2)}) copy-start(s32[128,8]{0,1:T(8,128)} %param.8) | copy-start | bytes 12292
  12.6 2.9 copy-start.8
  13.6 7.5 %collective-permute-start.1 = (bf16[896,384]{0,1:T(8,128)(2,1)}, bf16[896,384]{0,1:T(8,128)(2,1)}, u32[]{:S(2)}, u32[]{:S(2)}) collective-permute-start(bf16[896,384]{0,1:T(8,128)(2,1)} %broadcast_select_fusion.7), channel_id=1, source_target_pairs={{0,1},{1,0},{2,3},{3,2},{4,5},{5,4},{6,7},{7,6},{8,9},{9,8},{10,11... | collective-permute-start | bytes 2064392 | tf_op jit(solution)/shard_map/ppermute | solution.py:16
  18.3 1.9 copy-start.5
  20.2 5.3 %collective-permute-start.4 = (bf16[40,3584]{1,0:T(8,128)(2,1)}, bf16[40,3584]{1,0:T(8,128)(2,1)}, u32[]{:S(2)}, u32[]{:S(2)}) collective-permute-start(bf16[40,3584]{1,0:T(8,128)(2,1)} %bitcast.43), channel_id=1, source_target_pairs={{0,1},{1,0},{2,3},{3,2},{4,5},{5,4},{6,7},{7,6},{8,9},{9,8},{10,11... | collective-permute-start | bytes 860168 | tf_op jit(solution)/shard_map/ppermute | solution.py:16
  24.8 1.8 collective-permute-start
  29.3 53.6 %all-to-all-start = ((bf16[4,80,3584]{2,1,0:T(8,128)(2,1)}), bf16[4,80,3584]{2,1,0:T(8,128)(2,1)}, u32[]{:S(2)}, u32[]{:S(2)}) async-start(bf16[4,80,3584]{2,1,0:T(8,128)(2,1)} %broadcast_in_dim.42), calls=%async_computation | async-start | bytes 4587520 | tf_op jit(solution)/shard_map/all_to_all | solution.py:114
  84.4 55.8 %all-to-all-start.2 = ((bf16[4,80,3584]{2,1,0:T(8,128)(2,1)}), bf16[4,80,3584]{2,1,0:T(8,128)(2,1)}, u32[]{:S(2)}, u32[]{:S(2)}) async-start(bf16[4,80,3584]{2,1,0:T(8,128)(2,1)} %broadcast_in_dim.44), calls=%async_computation.2 | async-start | bytes 4587520 | tf_op jit(solution)/shard_map/all_to_all | solution.py:114
  92.1 193.5 %reduce-scatter.4.cloned.1.call-start = ((), (), s32[]{:S(2)}) async-start(), calls=%async_computation.6 | async-start | bytes 6881280
  96.3 49.3 %collective-permute-start.2 = (f32[320,512]{1,0:T(8,128)S(1)}, f32[320,512]{1,0:T(8,128)S(1)}, u32[]{:S(2)}, u32[]{:S(2)}) collective-permute-start(f32[320,512]{1,0:T(8,128)S(1)} %fusion.2), channel_id=1, source_target_pairs={{0,1},{1,0},{2,3},{3,2},{4,5},{5,4},{6,7},{7,6},{8,9},{9,8},{10,11... | collective-permute-start | bytes 1966088 | tf_op jit(solution)/shard_map/ppermute | solution.py:16
  143.2 3.6 %collective-permute-start.5 = (f32[320,256]{1,0:T(8,128)S(1)}, f32[320,256]{1,0:T(8,128)S(1)}, u32[]{:S(2)}, u32[]{:S(2)}) collective-permute-start(f32[320,256]{1,0:T(8,128)S(1)} %fusion.7), channel_id=1, source_target_pairs={{0,1},{1,0},{2,3},{3,2},{4,5},{5,4},{6,7},{7,6},{8,9},{9,8},{10,11... | collective-permute-start | bytes 983048 | tf_op jit(solution)/shard_map/ppermute | solution.py:16
  168.0 56.9 %all-to-all-start.1 = ((bf16[4,80,3584]{2,1,0:T(8,128)(2,1)}), bf16[4,80,3584]{2,1,0:T(8,128)(2,1)}, u32[]{:S(2)}, u32[]{:S(2)}) async-start(bf16[4,80,3584]{2,1,0:T(8,128)(2,1)} %bitcast.80), calls=%async_computation.1 | async-start | bytes 4587520 | tf_op jit(solution)/shard_map/all_to_all | solution.py:119
  224.9 55.8 %all-to-all-start.3 = ((bf16[4,80,3584]{2,1,0:T(8,128)(2,1)}), bf16[4,80,3584]{2,1,0:T(8,128)(2,1)}, u32[]{:S(2)}, u32[]{:S(2)}) async-start(bf16[4,80,3584]{2,1,0:T(8,128)(2,1)} %bitcast.87), calls=%async_computation.3 | async-start | bytes 4587520 | tf_op jit(solution)/shard_map/all_to_all | solution.py:119
  235.2 54.7 %collective-permute-start.3 = (bf16[40,3584]{1,0:T(8,128)(2,1)}, bf16[40,3584]{1,0:T(8,128)(2,1)}, u32[]{:S(2)}, u32[]{:S(2)}) collective-permute-start(bf16[40,3584]{1,0:T(8,128)(2,1)} %select_bitcast_fusion.3), channel_id=1, source_target_pairs={{0,1},{1,0},{2,3},{3,2},{4,5},{5,4},{6,7},{7,6},{8,9},{9,8},{10,11... | collective-permute-start | bytes 860168 | tf_op jit(solution)/shard_map/ppermute | solution.py:16
  283.5 15.4 %collective-permute-start.6 = (bf16[40,3584]{1,0:T(8,128)(2,1)}, bf16[40,3584]{1,0:T(8,128)(2,1)}, u32[]{:S(2)}, u32[]{:S(2)}) collective-permute-start(bf16[40,3584]{1,0:T(8,128)(2,1)} %select_bitcast_fusion), channel_id=1, source_target_pairs={{0,1},{1,0},{2,3},{3,2},{4,5},{5,4},{6,7},{7,6},{8,9},{9,8},{10,11... | collective-permute-start | bytes 860168 | tf_op jit(solution)/shard_map/ppermute | solution.py:16
  286.9 3.0 copy-start.3
  288.6 2.4 copy-start.4
  289.9 5.0 %collective-permute-start.7 = (bf16[896,384]{0,1:T(8,128)(2,1)}, bf16[896,384]{0,1:T(8,128)(2,1)}, u32[]{:S(2)}, u32[]{:S(2)}) collective-permute-start(bf16[896,384]{0,1:T(8,128)(2,1)} %broadcast_select_fusion.2), channel_id=1, source_target_pairs={{0,1},{1,0},{2,3},{3,2},{4,5},{5,4},{6,7},{7,6},{8,9},{9,8},{10,11... | collective-permute-start | bytes 2064392 | tf_op jit(solution)/shard_map/ppermute | solution.py:16
  294.8 2.0 copy-start.6
  294.8 2.1 copy-start.2
  298.4 9.0 %collective-permute-start.8 = (bf16[1792,384]{0,1:T(8,128)(2,1)}, bf16[1792,384]{0,1:T(8,128)(2,1)}, u32[]{:S(2)}, u32[]{:S(2)}) collective-permute-start(bf16[1792,384]{0,1:T(8,128)(2,1)} %fusion.6), channel_id=1, source_target_pairs={{0,1},{1,0},{2,3},{3,2},{4,5},{5,4},{6,7},{7,6},{8,9},{9,8},{10,11... | collective-permute-start | bytes 4128776 | tf_op jit(solution)/shard_map/ppermute | solution.py:16
  302.0 8.0 %copy-start.1 = (bf16[128,7168]{1,0:T(8,128)(2,1)S(1)}, bf16[128,7168]{1,0:T(8,128)(2,1)}, u32[]{:S(2)}) copy-start(bf16[128,7168]{1,0:T(8,128)(2,1)} %param.7) | copy-start | bytes 5505028
Sparse Core Ops, SparseCore 0:
  23.8 64.2 all-gather.1
  164.5 64.9 reduce-scatter.3

commit v2 on v1

--- a/solution.py
+++ b/solution.py
@@ -1,6 +1,10 @@
+import functools
+
 import jax
 import jax.numpy as jnp
 from jax import lax
+from jax.experimental import pallas as pl
+from jax.experimental.pallas import tpu as pltpu
 from jax.sharding import Mesh
 from jax.sharding import PartitionSpec as P
 
@@ -43,6 +47,217 @@
         preferred_element_type=jnp.float32,
         precision=precision,
     )
+
+
+def greet_line(me, chips):
+    barrier = pltpu.get_barrier_semaphore()
+    for cond, peer in ((me < chips - 1, me + 1), (me > 0, me - 1)):
+
+        @pl.when(cond)
+        def _():
+            pl.semaphore_signal(
+                barrier,
+                inc=1,
+                device_id={"sl": peer},
+                device_id_type=pl.DeviceIdType.MESH,
+            )
+
+    inner = (me > 0) & (me < chips - 1)
+    pl.semaphore_wait(barrier, jnp.where(inner, 2, 1))
+
+
+def gather_kernel(chips, *refs):
+    count = (len(refs) - 3) // 2
+    blocks, outs = refs[:count], refs[count : 2 * count]
+    own_sem, send_sem, recv_sem = refs[2 * count :]
+    me = lax.axis_index("sl")
+    greet_line(me, chips)
+
+    def copy(way, part, hop, source):
+        step = 1 - 2 * way
+        index = me - step * hop
+        return pltpu.make_async_remote_copy(
+            src_ref=source if source is not None else outs[part].at[index],
+            dst_ref=outs[part].at[index],
+            send_sem=send_sem.at[way, part, hop],
+            recv_sem=recv_sem.at[way, part, hop],
+            device_id={"sl": me + step},
+            device_id_type=pl.DeviceIdType.MESH,
+        )
+
+    def arrival(way, part, hop):
+        step = 1 - 2 * way
+        index = me - step * (hop + 1)
+        return pltpu.make_async_remote_copy(
+            src_ref=outs[part].at[index],
+            dst_ref=outs[part].at[index],
+            send_sem=send_sem.at[way, part, hop],
+            recv_sem=recv_sem.at[way, part, hop],
+            device_id={"sl": me - step},
+            device_id_type=pl.DeviceIdType.MESH,
+        )
+
+    def place(way):
+        return me if way == 0 else chips - 1 - me
+
+    for part in range(count):
+        for way in range(2):
+
+            @pl.when(place(way) < chips - 1)
+            def _():
+                copy(way, part, 0, blocks[part]).start()
+
+    owns = []
+    for part in range(count):
+        own = pltpu.make_async_copy(blocks[part], outs[part].at[me], own_sem.at[part])
+        own.start()
+        owns.append(own)
+    for hop in range(1, chips):
+        for part in range(count):
+            for way in range(2):
+
+                @pl.when(place(way) >= hop)
+                def _():
+                    arrival(way, part, hop - 1).wait_recv()
+
+                if hop < chips - 1:
+
+                    @pl.when((place(way) >= hop) & (place(way) < chips - 1))
+                    def _():
+                        copy(way, part, hop, None).start()
+
+    for own in owns:
+        own.wait()
+    for hop in range(chips - 1):
+        for part in range(count):
+            for way in range(2):
+
+                @pl.when((place(way) >= hop) & (place(way) < chips - 1))
+                def _():
+                    copy(way, part, hop, blocks[part] if hop == 0 else None).wait_send()
+
+
+def line_gather(chips, blocks):
+    rows, columns = blocks[0].shape
+    count = len(blocks)
+    return pl.pallas_call(
+        functools.partial(gather_kernel, chips),
+        out_shape=[jax.ShapeDtypeStruct((chips, rows, columns), b.dtype) for b in blocks],
+        in_specs=[pl.BlockSpec(memory_space=pltpu.VMEM)] * count,
+        out_specs=[pl.BlockSpec(memory_space=pl.ANY)] * count,
+        scratch_shapes=[
+            pltpu.SemaphoreType.DMA((count,)),
+            pltpu.SemaphoreType.DMA((2, count, chips - 1)),
+            pltpu.SemaphoreType.DMA((2, count, chips - 1)),
+        ],
+        compiler_params=pltpu.CompilerParams(collective_id=0, has_side_effects=True),
+        name="line_gather",
+    )(*blocks)
+
+
+def reduce_kernel(chips, *refs):
+    count = (len(refs) - 4) // 2
+    parts, outs = refs[:count], refs[count : 2 * count]
+    landed, sums, send_sem, recv_sem = refs[2 * count :]
+    me = lax.axis_index("sl")
+    greet_line(me, chips)
+
+    def place(way):
+        return me if way == 0 else chips - 1 - me
+
+    def target(way, slot):
+        return chips - 1 - slot if way == 0 else slot
+
+    def copy(way, part, slot, source):
+        return pltpu.make_async_remote_copy(
+            src_ref=source,
+            dst_ref=landed.at[way, part, slot],
+            send_sem=send_sem.at[way, part, slot],
+            recv_sem=recv_sem.at[way, part, slot],
+            device_id={"sl": me + 1 - 2 * way},
+            device_id_type=pl.DeviceIdType.MESH,
+        )
+
+    def arrival(way, part, slot):
+        return pltpu.make_async_remote_copy(
+            src_ref=landed.at[way, part, slot],
+            dst_ref=landed.at[way, part, slot],
+            send_sem=send_sem.at[way, part, slot],
+            recv_sem=recv_sem.at[way, part, slot],
+            device_id={"sl": me - 1 + 2 * way},
+            device_id_type=pl.DeviceIdType.MESH,
+        )
+
+    for slot in range(chips - 1):
+        for part in range(count):
+            for way in range(2):
+
+                @pl.when(place(way) == 0)
+                def _():
+                    copy(way, part, slot, parts[part].at[target(way, slot)]).start()
+
+    for slot in range(chips - 2):
+        for part in range(count):
+            for way in range(2):
+
+                @pl.when((place(way) > 0) & (place(way) < chips - 1 - slot))
+                def _():
+                    arrival(way, part, slot).wait_recv()
+                    sums[way, part, slot] = (
+                        landed[way, part, slot].astype(jnp.float32)
+                        + parts[part][target(way, slot)].astype(jnp.float32)
+                    ).astype(sums.dtype)
+                    copy(way, part, slot, sums.at[way, part, slot]).start()
+
+    for part in range(count):
+        for here in range(chips):
+
+            @pl.when(me == here)
+            def _():
+                total = parts[part][here].astype(jnp.float32)
+                if here > 0:
+                    arrival(0, part, chips - 1 - here).wait_recv()
+                    total = total + landed[0, part, chips - 1 - here].astype(jnp.float32)
+                if here < chips - 1:
+                    arrival(1, part, here).wait_recv()
+                    total = total + landed[1, part, here].astype(jnp.float32)
+                outs[part][...] = total.astype(outs[part].dtype)
+
+    for slot in range(chips - 1):
+        for part in range(count):
+            for way in range(2):
+
+                @pl.when(place(way) == 0)
+                def _():
+                    copy(way, part, slot, parts[part].at[target(way, slot)]).wait_send()
+
+                if slot < chips - 2:
+
+                    @pl.when((place(way) > 0) & (place(way) < chips - 1 - slot))
+                    def _():
+                        copy(way, part, slot, sums.at[way, part, slot]).wait_send()
+
+
+def line_reduce(chips, parts):
+    _, rows, columns = parts[0].shape
+    count = len(parts)
+    kind = parts[0].dtype
+    return pl.pallas_call(
+        functools.partial(reduce_kernel, chips),
+        out_shape=[jax.ShapeDtypeStruct((rows, columns), kind)] * count,
+        in_specs=[pl.BlockSpec(memory_space=pltpu.VMEM)] * count,
+        out_specs=[pl.BlockSpec(memory_space=pltpu.VMEM)] * count,
+        scratch_shapes=[
+            pltpu.VMEM((2, count, chips - 1, rows, columns), kind),
+            pltpu.VMEM((2, count, chips - 2, rows, columns), kind),
+            pltpu.SemaphoreType.DMA((2, count, chips - 1)),
+            pltpu.SemaphoreType.DMA((2, count, chips - 1)),
+        ],
+        compiler_params=pltpu.CompilerParams(
+            collective_id=1, has_side_effects=True, vmem_limit_bytes=48 * 1024 * 1024
+        ),
+        name="line_reduce",
+    )(*parts)
 
 
 def local(tokens, cotangent, route_ids, router_weights, master, accumulator):
@@ -99,7 +314,7 @@
     token_rows = dot(select, tokens, 0, 0).astype(bf16)
     grad_rows = (dot(select, cotangent, 0, 0) * slot_weight[:, None]).astype(bf16)
 
-    def gather(rows):
+    def pair_block(rows):
         own, other = split_cols(rows)
         block = ordered(
             core,
@@ -109,15 +324,9 @@
         )
         if live_count > 1:
             block = lax.all_to_all(block, "ex", split_axis=0, concat_axis=0, tiled=True)
-        block = block.reshape(1, live_count * CORES * capacity, half_width)
-        tiled = jnp.broadcast_to(block, (chips,) + block.shape[1:])
-        full = lax.all_to_all(tiled, "sl", split_axis=0, concat_axis=0, tiled=True)
-        return full.reshape(-1, half_width)
-
-    def give_back(part):
-        blocks = part.reshape(chips, live_count * CORES * capacity, half_width)
-        back = lax.all_to_all(blocks, "sl", split_axis=0, concat_axis=0, tiled=True)
-        summed = jnp.sum(back.astype(jnp.float32), axis=0).astype(bf16)
+        return block.reshape(live_count * CORES * capacity, half_width)
+
+    def give_back(summed):
         summed = summed.reshape(live_count, CORES, capacity, half_width)
         if live_count > 1:
             summed = lax.all_to_all(summed, "ex", split_axis=0, concat_axis=0, tiled=True)
@@ -127,8 +336,9 @@
         other = swap(jnp.where(core == 0, high, low))
         return join_cols(own, other)
 
-    in_rows = gather(token_rows)
-    cot_rows = gather(grad_rows)
+    in_rows, cot_rows = line_gather(chips, [pair_block(token_rows), pair_block(grad_rows)])
+    in_rows = in_rows.reshape(-1, half_width)
+    cot_rows = cot_rows.reshape(-1, half_width)
 
     gate_up_part = dot(in_rows, w_in, 1, 0)
     gate_up = gate_up_part + swap(gate_up_part)
@@ -142,7 +352,6 @@
     silu_gate = gate_pre * sigmoid_gate
     hidden = (silu_gate * up_pre).astype(bf16)
     out_part = dot(hidden, w_down, 1, 1).astype(bf16)
-    out_rows = give_back(out_part)
 
     grad_hidden_part = dot(cot_rows, w_down, 1, 0)
     grad_hidden = grad_hidden_part + swap(grad_hidden_part)
@@ -158,7 +367,6 @@
         axis=1,
     ).astype(bf16)
     in_part = dot(grad_pre, w_in, 1, 1).astype(bf16)
-    back_rows = give_back(in_part)
 
     grad_in = dot(in_rows, grad_pre, 0, 0).astype(bf16)
     grad_down = dot(cot_rows, hidden, 0, 0).astype(bf16)
@@ -168,6 +376,10 @@
         scatter_dimension=0,
         tiled=True,
     )
+    blocks = (chips, live_count * CORES * capacity, half_width)
+    out_sum, in_sum = line_reduce(chips, [out_part.reshape(blocks), in_part.reshape(blocks)])
+    out_rows = give_back(out_sum)
+    back_rows = give_back(in_sum)
     low = jnp.concatenate(
         [summed[:, :two], summed[:, 2 * two : 2 * two + slice_width]], axis=1
     )

time: 322 us -> 259 us (0.80); the launches traced: 317 us -> 258 us
  waiting for transfers between devices: 182 us -> 4.48 us
  Pallas kernels: 0 us -> 168 us
  starting transfers between devices: 37.2 us -> 6.38 us
  matrix products: 28.5 us -> 21.1 us
  other arithmetic: 26.3 us -> 20 us
  local copies, waits for them, and re-layouts: 28.8 us -> 23.6 us
    all_to_all x4 -> x0, waiting for transfers between devices: 179 us -> none  [the longest x2 91 us: gather(): full = lax.all_to_all(tiled, 'sl', split_axis=0, concat_axis=0, tiled=True)]
    pallas_call x0 -> x2, Pallas kernels: none -> 168 us  [the longest x1 91.5 us: line_reduce(): pl.pallas_call(functools.partial(reduce_kernel, chips), out_shape=[jax.Sh...]
    all_to_all x4 -> x0, starting transfers between devices: 27.7 us -> none  [the longest x2 15.3 us: give_back(): back = lax.all_to_all(blocks, 'sl', split_axis=0, concat_axis=0, tiled=True)]
    dot_general x10, matrix products: 28.5 us -> 21.1 us  [dot(): lax.dot_general(left, right, (((left_dim,), (right_dim,)), ((), ())), pre...]
    reduce_sum x2 -> x0, other arithmetic: 4.09 us -> none  [give_back(): summed = jnp.sum(back.astype(jnp.float32), axis=0).astype(bf16)]
    unnamed x29 -> x31, local copies, waits for them, and re-layouts: 15.7 us -> 15.8 us
  transfers between devices with their start and end apart: 15 -> 11, of which waited for: 6 -> 3; matrix products, arithmetic and copies ran while one was open for 18% -> 14% of each run, Pallas kernels for 0% -> 65%
where the time goes in v2:
time: 259 us; the launch traced here: 258 us
  Pallas kernels  168 us (65%)
  local copies, waits for them, and re-layouts  23.6 us (9%)
  matrix products  21.1 us (8%)
  other arithmetic  20 us (8%)
  between operations  14.5 us (6%)
  starting transfers between devices  6.38 us (2%)
  waiting for transfers between devices  4.48 us (2%)
    pallas_call x1, Pallas kernels, line_reduce(): pl.pallas_call(functools.partial(reduce_kernel, chips), out_shape=[jax.Sh...  91.5 us
    pallas_call x1, Pallas kernels, line_gather(): pl.pallas_call(functools.partial(gather_kernel, chips), out_shape=[jax.Sh...  76.5 us
    dot_general x10, matrix products, dot(): lax.dot_general(left, right, (((left_dim,), (right_dim,)), ((), ())), pre...  21.1 us
    unnamed x31, local copies, waits for them, and re-layouts  15.8 us
    ppermute x9, starting transfers between devices, swap(): return lax.ppermute(array, 'core', [(0, 1), (1, 0)])  6.3 us
  transfers between devices with their start and end apart: 11, of which 3 were waited for; matrix products, arithmetic and copies ran while one was open for 14% of the time, Pallas kernels for 65%

profile of v2, /device:TPU:9, one launch (start us, length us, event | category | flops | bytes accessed | tf_op | source)
XLA Modules:
  0.0 258.1 jit_solution(17576460717583537101)
XLA Ops:
  7.2 3.5 %copy.77 = f32[1,1792,384]{1,2,0:T(8,128)} copy(f32[1,1792,384]{2,1,0:T(8,128)} %param.10) | data formatting | bytes 5505024 | tf_op args[4]
  10.7 1.9 bitcast_convert_fusion
  12.7 0.7 collective-permute-start.2
  13.5 1.8 collective-permute-done.2
  15.2 0.2 broadcast_select_fusion.5
  15.6 1.2 pad_maximum_fusion.1
  17.1 0.3 reduce-window.6
  17.5 0.2 slice_reduce_fusion
  17.7 0.2 reduce-window.9
  18.3 0.4 fusion
  18.7 0.4 reshape.177
  19.1 0.8 fusion.22
  19.9 0.3 broadcast_select_fusion.9
  20.3 0.4 collective-permute-start.1
  20.7 0.4 convolution_convert_fusion.2
  21.1 0.4 reshape.175
  21.6 0.8 fusion.23
  22.4 0.3 broadcast_select_fusion.11
  22.7 0.3 collective-permute-start
  23.1 1.2 collective-permute-done
  24.4 0.9 pad_maximum_fusion.4
  25.3 0.9 pad_maximum_fusion.5
  26.2 76.5 %line_gather.1 = (bf16[4,80,3584]{2,1,0:T(8,128)(2,1)}, bf16[4,80,3584]{2,1,0:T(8,128)(2,1)}) custom-call(bf16[80,3584]{1,0:T(8,128)(2,1)} %bitcast.90, bf16[80,3584]{1,0:T(8,128)(2,1)} %bitcast.91), custom_call_target="tpu_custom_call" | custom-call | tf_op jit(solution)/shard_map/line_gather/pallas_call | solution.py:143
  102.7 4.2 %fusion.2 = f32[320,512]{1,0:T(8,128)S(1)} fusion(bf16[320,3584]{1,0:T(8,128)(2,1)} %bitcast.101, bf16[3584,768]{0,1:T(8,128)(2,1)} %all-gather.2.cloned.1.call-done), kind=kOutput, calls=%fused_computation.11 | convolution fusion | flops 1174405120 | bytes 6619136 | tf_op jit(solution)/shard_map/dot_general | solution.py:43
  107.0 1.2 collective-permute-start.3
  108.2 2.3 fusion.7
  110.8 1.4 collective-permute-done.4
  112.2 0.2 multiply_convert_fusion.1
  112.4 1.2 convolution_convert_fusion.6
  113.6 0.5 copy-done.9
  114.1 2.1 convolution_convert_fusion.3
  116.2 2.7 %pad_maximum_fusion = bf16[3584,768]{0,1:T(8,128)(2,1)} fusion(bf16[3584,256]{0,1:T(8,128)(2,1)S(1)} %convolution_convert_fusion.6, bf16[3584,512]{0,1:T(8,128)(2,1)S(1)} %convolution_convert_fusion.3), kind=kLoop, calls=%fused_computation.6 | loop fusion | flops 11010048 | bytes 11010048 | tf_op jit(solution)/shard_map/concatenate | solution.py:374
  118.9 8.3 %copy.83 = bf16[3584,768]{1,0:T(8,128)(2,1)} copy(bf16[3584,768]{0,1:T(8,128)(2,1)} %pad_maximum_fusion) | data formatting | bytes 11010048
  127.2 2.3 convolution_convert_fusion.5
  129.5 3.4 %convolution_convert_fusion.4 = bf16[320,3584]{1,0:T(8,128)(2,1)S(1)} fusion(bf16[3584,768]{0,1:T(8,128)(2,1)} %all-gather.2.cloned.1.call-done, bf16[320,128]{1,0:T(8,128)(2,1)S(1)} %get-tuple-element.70, bf16[320,128]{1,0:T(8,128)(2,1)S(1)} %get-tuple-element.68, bf16[320,128]{1,0:T(8,128)(2,1)S(1)} %get-tuple-element.69, ...), kind=kOutput, calls=%fused_computation.7 | convolution fusion | flops 1176862720 | bytes 6291456 | tf_op jit(solution)/shard_map/dot_general | solution.py:43
  132.9 91.5 %line_reduce.1 = (bf16[80,3584]{1,0:T(8,128)(2,1)S(1)}, bf16[80,3584]{1,0:T(8,128)(2,1)S(1)}) custom-call(bf16[4,80,3584]{2,1,0:T(8,128)(2,1)S(1)} %bitcast.80, bf16[4,80,3584]{2,1,0:T(8,128)(2,1)S(1)} %bitcast.85), custom_call_target="tpu_custom_call" | custom-call | tf_op jit(solution)/shard_map/line_reduce/pallas_call | solution.py:245
  224.3 0.7 select_bitcast_fusion.1
  225.1 3.0 %collective-permute-start.5 = (bf16[40,3584]{1,0:T(8,128)(2,1)}, bf16[40,3584]{1,0:T(8,128)(2,1)}, u32[]{:S(2)}, u32[]{:S(2)}) collective-permute-start(bf16[40,3584]{1,0:T(8,128)(2,1)} %select_bitcast_fusion.1), channel_id=1, source_target_pairs={{0,1},{1,0},{2,3},{3,2},{4,5},{5,4},{6,7},{7,6},{8,9},{9,8},{10,11... | collective-permute-start | bytes 860168 | tf_op jit(solution)/shard_map/ppermute | solution.py:20
  228.1 0.7 select_bitcast_fusion
  228.9 1.1 fusion.20
  229.9 0.2 copy.93
  230.1 1.2 fusion.19
  231.3 0.2 copy.92
  231.6 0.2 copy.91
  231.8 0.2 copy.90
  232.0 1.0 broadcast_select_fusion.2
  233.0 0.5 collective-permute-start.7
  233.5 1.0 bitcast_select_fusion.3
  234.6 0.1 reshape.193
  234.7 0.1 reshape.192
  234.9 1.3 pad_maximum_fusion.6
  236.2 0.4 reshape.186
  236.6 1.6 broadcast_select_fusion.1
  238.3 0.3 multiply_reduce_fusion
  238.7 1.5 fusion.6
  240.2 1.0 bitcast_select_fusion.1
  241.2 0.1 reshape.195
  241.3 0.1 reshape.194
  241.5 1.3 pad_maximum_fusion.7
  242.8 0.4 reshape.190
  243.3 1.9 convolution_convert_fusion
  245.2 2.9 %convolution_convert_fusion.1 = bf16[128,7168]{1,0:T(8,128)(2,1)} fusion(bf16[40,7168]{1,0:T(8,128)(2,1)S(1)} %reshape.186, f32[128,40]{0,1:T(8,128)S(1)} %get-tuple-element.33, f32[40]{0:T(128)S(1)} %get-tuple-element.32), kind=kOutput, calls=%fused_computation.1 | convolution fusion | flops 441324544 | bytes 2429088 | tf_op jit(solution)/shard_map/dot_general | solution.py:43
  248.1 0.6 broadcast_in_dim.28
  248.7 2.5 copy.82
  (60 shorter events, 1.7 us)
Async XLA Ops:
  7.2 11.1 %copy-start = (bf16[128,7168]{1,0:T(8,128)(2,1)S(1)}, bf16[128,7168]{1,0:T(8,128)(2,1)}, u32[]{:S(2)}) copy-start(bf16[128,7168]{1,0:T(8,128)(2,1)} %param.7) | copy-start | bytes 5505028
  7.2 95.5 %all-gather.2.cloned.1.call-start = ((), (), s32[]{:S(2)}) async-start(), calls=%async_computation.1 | async-start | bytes 6881280 | tf_op jit(solution)/shard_map/all_gather | solution.py:306
  12.7 2.5 collective-permute-start.2
  15.6 1.3 copy-start.7
  15.6 2.6 copy-start.8
  16.8 212.0 %reduce-scatter.4.cloned.1.call-start = ((), (), s32[]{:S(2)}) async-start(), calls=%async_computation.2 | async-start | bytes 6881280
  19.1 1.6 copy-start.5
  20.3 2.8 %collective-permute-start.1 = (bf16[40,3584]{1,0:T(8,128)(2,1)S(1)}, bf16[40,3584]{1,0:T(8,128)(2,1)S(1)}, u32[]{:S(2)}, u32[]{:S(2)}) collective-permute-start(bf16[40,3584]{1,0:T(8,128)(2,1)S(1)} %bitcast.98), channel_id=1, source_target_pairs={{0,1},{1,0},{2,3},{3,2},{4,5},{5,4},{6,7},{7,6},{8,9},{9,8},{10,11... | collective-permute-start | bytes 860168 | tf_op jit(solution)/shard_map/ppermute | solution.py:20
  22.7 1.6 collective-permute-start
  102.7 5.5 %copy-start.3 = (bf16[4,80,3584]{2,1,0:T(8,128)(2,1)S(1)}, bf16[4,80,3584]{2,1,0:T(8,128)(2,1)}, u32[]{:S(2)}) copy-start(bf16[4,80,3584]{2,1,0:T(8,128)(2,1)} %get-tuple-element.9) | copy-start | bytes 6881284
  107.0 3.6 %collective-permute-start.3 = (f32[320,512]{1,0:T(8,128)S(1)}, f32[320,512]{1,0:T(8,128)S(1)}, u32[]{:S(2)}, u32[]{:S(2)}) collective-permute-start(f32[320,512]{1,0:T(8,128)S(1)} %fusion.2), channel_id=1, source_target_pairs={{0,1},{1,0},{2,3},{3,2},{4,5},{5,4},{6,7},{7,6},{8,9},{9,8},{10,11... | collective-permute-start | bytes 1966088 | tf_op jit(solution)/shard_map/ppermute | solution.py:20
  110.5 1.7 collective-permute-start.4
  112.4 1.6 copy-start.9
  225.1 8.5 %collective-permute-start.5 = (bf16[40,3584]{1,0:T(8,128)(2,1)}, bf16[40,3584]{1,0:T(8,128)(2,1)}, u32[]{:S(2)}, u32[]{:S(2)}) collective-permute-start(bf16[40,3584]{1,0:T(8,128)(2,1)} %select_bitcast_fusion.1), channel_id=1, source_target_pairs={{0,1},{1,0},{2,3},{3,2},{4,5},{5,4},{6,7},{7,6},{8,9},{9,8},{10,11... | collective-permute-start | bytes 860168 | tf_op jit(solution)/shard_map/ppermute | solution.py:20
  228.8 11.3 %collective-permute-start.6 = (bf16[40,3584]{1,0:T(8,128)(2,1)}, bf16[40,3584]{1,0:T(8,128)(2,1)}, u32[]{:S(2)}, u32[]{:S(2)}) collective-permute-start(bf16[40,3584]{1,0:T(8,128)(2,1)} %select_bitcast_fusion), channel_id=1, source_target_pairs={{0,1},{1,0},{2,3},{3,2},{4,5},{5,4},{6,7},{7,6},{8,9},{9,8},{10,11... | collective-permute-start | bytes 860168 | tf_op jit(solution)/shard_map/ppermute | solution.py:20
  231.8 2.9 %copy-start.4 = (bf16[896,128]{0,1:T(8,128)(2,1)}, bf16[896,128]{0,1:T(8,128)(2,1)S(1)}, u32[]{:S(2)}) copy-start(bf16[896,128]{0,1:T(8,128)(2,1)S(1)} %copy.91) | copy-start | bytes 688132
  233.0 3.6 %collective-permute-start.7 = (bf16[896,384]{0,1:T(8,128)(2,1)}, bf16[896,384]{0,1:T(8,128)(2,1)}, u32[]{:S(2)}, u32[]{:S(2)}) collective-permute-start(bf16[896,384]{0,1:T(8,128)(2,1)} %broadcast_select_fusion.2), channel_id=1, source_target_pairs={{0,1},{1,0},{2,3},{3,2},{4,5},{5,4},{6,7},{7,6},{8,9},{9,8},{10,11... | collective-permute-start | bytes 2064392 | tf_op jit(solution)/shard_map/ppermute | solution.py:20
  236.6 2.0 copy-start.6
  236.6 2.1 copy-start.2
  240.2 8.5 %collective-permute-start.8 = (bf16[1792,384]{0,1:T(8,128)(2,1)}, bf16[1792,384]{0,1:T(8,128)(2,1)}, u32[]{:S(2)}, u32[]{:S(2)}) collective-permute-start(bf16[1792,384]{0,1:T(8,128)(2,1)} %fusion.6), channel_id=1, source_target_pairs={{0,1},{1,0},{2,3},{3,2},{4,5},{5,4},{6,7},{7,6},{8,9},{9,8},{10,11... | collective-permute-start | bytes 4128776 | tf_op jit(solution)/shard_map/ppermute | solution.py:20
  243.2 8.0 %copy-start.1 = (bf16[128,7168]{1,0:T(8,128)(2,1)S(1)}, bf16[128,7168]{1,0:T(8,128)(2,1)}, u32[]{:S(2)}) copy-start(bf16[128,7168]{1,0:T(8,128)(2,1)} %param.7) | copy-start | bytes 5505028
Sparse Core Ops, SparseCore 0:
  16.9 64.1 all-gather.1
  127.3 64.8 reduce-scatter.3
